TPU v7x, 1024 devices: a whole 4x4x32 slice. The times are simulated.
1024 devices in a mesh: bag: 64 (over z, core), head: 16 (over x, y).
Axes of the slice: x: 4, y: 4, z: 32, core: 2. Of those that a mesh axis runs over, the one named last changes fastest.
Arguments:
- projected: bfloat16 [131072, 3, 2048], P(('bag', 'head')), may hold values from -5.2 to 5.2
- video_ids: int32 [131072], P(('bag', 'head')), may hold values from 0 to 127, as said below
- bag_route: int32 [131072], P(('bag', 'head')), may hold values from 0 to 63, as said below
Outputs:
- attended: bfloat16 [131072, 2048], P(('bag', 'head'))
Inputs may be any that keep to these rules, and one draw needn't show every extreme that they name: `bag_route`: every device's 128 tokens name each bag exactly 2 times, so every bag receives 2048 tokens. `video_ids`: all tokens of a video have the same bag_route; the tokens of bag b belong to exactly 2 videos, numbered b * 2 to b * 2 + 1.
All inputs are finite; a program needn't handle non-finite values.
Results may differ from a plain program's by a relative error of at most 0.0046.
Values may be sent and summed in bfloat16 or wider, within the bound.
A program may use at most 64 MiB of HBM per device.

v0:
```python
import math

import jax
import jax.numpy as jnp
from jax import lax
from jax.sharding import PartitionSpec as P

HD = 128


def cut_along(array, dim, length):
    lengths = array.shape
    pieces = array.reshape(*lengths[:dim], length, lengths[dim] // length, *lengths[dim + 1 :])
    return jnp.moveaxis(pieces, dim, 0)


def in_order(pieces, dim):
    pieces = jnp.moveaxis(pieces, 0, dim)
    lengths = pieces.shape
    return pieces.reshape(*lengths[:dim], lengths[dim] * lengths[dim + 1], *lengths[dim + 2 :])


def joined_exchange(array, axis, axes, splits, concats):
    sizes = [lax.axis_size(a) for a in axes]
    pieces = cut_along(array, splits[0], sizes[0])
    pieces = jnp.moveaxis(cut_along(pieces, splits[1] + 1, sizes[1]), 0, 1)
    inside = pieces.shape[2:]
    pieces = pieces.reshape(-1, *inside)
    pieces = lax.all_to_all(pieces, axis, split_axis=0, concat_axis=0, tiled=True)
    pieces = in_order(pieces.reshape(*sizes, *inside), concats[0] + 1)
    return in_order(pieces, concats[1])


def masked_scores(query_rows, key_rows, query_ids, key_ids, scaling):
    scores = (
        jnp.einsum("qd,kd->qk", query_rows, key_rows, preferred_element_type=jnp.float32) * scaling
    )
    return jnp.where(query_ids[:, None] == key_ids[None, :], scores, -jnp.inf)


def attend_full(query_rows, key_rows, value_rows, row_ids, scaling):
    row_count = query_rows.shape[0]
    block_rows = 512
    blocks = row_count // block_rows

    def one_block(inputs):
        query_block, id_block = inputs
        scores = masked_scores(query_block, key_rows, id_block, row_ids, scaling)
        row_max = jnp.max(scores, axis=1, keepdims=True)
        weights = jnp.exp(scores - row_max)
        row_total = jnp.sum(weights, axis=1, keepdims=True)
        mixed_sum = jnp.dot(
            weights.astype(jnp.bfloat16), value_rows, preferred_element_type=jnp.float32
        )
        return (mixed_sum / row_total).astype(jnp.bfloat16)

    result = lax.map(
        one_block, (query_rows.reshape(blocks, block_rows, -1), row_ids.reshape(blocks, block_rows))
    )
    return result.reshape(row_count, -1)


def local(projected, video_ids, bag_route):
    local_rows = projected.shape[0]
    feature_width = projected.shape[2]
    bag_count = lax.axis_size("bag")
    head_count = lax.axis_size("head")
    per_bag = local_rows // bag_count
    head_width = feature_width // head_count
    heads_here = head_width // HD
    scaling = 1.0 / math.sqrt(HD)
    ordering = jnp.argsort(bag_route, stable=True)
    grouped = projected[ordering].reshape(bag_count, per_bag, 3, head_count, head_width)
    grouped_ids = jnp.broadcast_to(
        video_ids[ordering].reshape(bag_count, per_bag, 1, 1), (bag_count, per_bag, 1, head_count)
    )
    arrived, arrived_ids = (
        lax.all_to_all(
            lax.all_to_all(grouped, "bag", split_axis=0, concat_axis=0, tiled=True),
            "head",
            split_axis=3,
            concat_axis=1,
            tiled=True,
        ),
        lax.all_to_all(
            lax.all_to_all(grouped_ids, "bag", split_axis=0, concat_axis=0, tiled=True),
            "head",
            split_axis=3,
            concat_axis=1,
            tiled=True,
        ),
    )
    row_ids = arrived_ids.reshape(-1)
    bag_rows = row_ids.shape[0]
    per_head = jnp.moveaxis(arrived.reshape(bag_rows, 3, heads_here, HD), 2, 0)

    def one_head(stacked):
        return attend_full(stacked[:, 0], stacked[:, 1], stacked[:, 2], row_ids, scaling)

    attended_heads = lax.map(one_head, per_head)
    result = jnp.moveaxis(attended_heads, 0, 1).reshape(bag_rows, head_width)
    home_rows = joined_exchange(
        result.reshape(bag_count, head_count * per_bag, 1, head_width),
        ("bag", "head"),
        ("bag", "head"),
        (0, 1),
        (0, 2),
    )
    return home_rows.reshape(local_rows, feature_width)[jnp.argsort(ordering)]


def solution(mesh):
    placed = (P(("bag", "head"), None, None), P(("bag", "head")), P(("bag", "head")))
    return jax.shard_map(
        local, mesh=mesh, in_specs=placed, out_specs=P(("bag", "head"), None), check_vma=False
    )
```

profile of v0, /device:TPU:1, one launch (start us, length us, event | category | flops | bytes accessed | tf_op | source)
XLA Modules:
  0.0 354.2 jit_solution(10120831298698921488)
XLA Ops:
  0.0 3.3 sort.34
  3.3 1.6 gather_fusion
  5.1 0.8 broadcast_in_dim.31
  5.8 30.4 %all-to-all-start = ((s32[64,2,1,16]{3,1,2,0:T(2,128)}), s32[64,2,1,16]{3,1,2,0:T(2,128)S(1)}, u32[]{:S(2)}, u32[]{:S(2)}) async-start(s32[64,2,1,16]{3,1,2,0:T(2,128)} %broadcast_in_dim.31), calls=%async_computation | async-start | bytes 131072 | tf_op jit(solution)/shard_map/all_to_all | solution.py:86
  36.2 5.2 %gather_fusion.1 = bf16[128,3,2048]{2,0,1:T(8,128)(2,1)S(1)} fusion(bf16[128,3,2048]{2,0,1:T(8,128)(2,1)S(1)} %copy-done, s32[1024]{0:T(1024)S(1)} %pad_clamp_fusion.1), kind=kCustom, calls=%fused_computation.1 | custom fusion | bytes 3146240 | tf_op jit(solution)/shard_map/gather | solution.py:73
  41.9 1.4 copy.34
  43.3 18.1 %all-to-all-done = s32[64,2,1,16]{3,1,2,0:T(2,128)S(1)} async-done(((s32[64,2,1,16]{3,1,2,0:T(2,128)}), s32[64,2,1,16]{3,1,2,0:T(2,128)S(1)}, u32[]{:S(2)}, u32[]{:S(2)}) %all-to-all-start) | async-done | bytes 8224 | tf_op jit(solution)/shard_map/all_to_all | solution.py:86
  61.4 5.8 %all-to-all-start.2 = ((bf16[64,2,3,16,128]{4,3,1,2,0:T(8,128)(2,1)}), bf16[64,2,3,16,128]{4,3,1,2,0:T(8,128)(2,1)S(1)}, u32[]{:S(2)}, u32[]{:S(2)}) async-start(bf16[64,2,3,16,128]{4,3,1,2,0:T(8,128)(2,1)} %copy.34), calls=%async_computation.2 | async-start | bytes 3145728 | tf_op jit(solution)/shard_map/all_to_all | solution.py:79
  67.9 151.1 %all-to-all-done.2 = bf16[64,2,3,16,128]{4,3,1,2,0:T(8,128)(2,1)S(1)} async-done(((bf16[64,2,3,16,128]{4,3,1,2,0:T(8,128)(2,1)}), bf16[64,2,3,16,128]{4,3,1,2,0:T(8,128)(2,1)S(1)}, u32[]{:S(2)}, u32[]{:S(2)}) %all-to-all-start.2) | async-done | bytes 1572896 | tf_op jit(solution)/shard_map/all_to_all | solution.py:79
  219.0 6.8 %all-to-all-start.1 = ((s32[16,1,128]{2,1,0:T(1,128)}), s32[16,1,128]{2,1,0:T(1,128)S(1)}, u32[]{:S(2)}, u32[]{:S(2)}) async-start(s32[16,1,128]{2,1,0:T(1,128)} %reshape.55), calls=%async_computation.1 | async-start | bytes 16384 | tf_op jit(solution)/shard_map/all_to_all | solution.py:85
  225.8 2.9 copy.35
  228.6 3.5 all-to-all-done.1
  232.1 3.9 %all-to-all-start.3 = ((bf16[64,2,3,16,128]{4,1,0,2,3:T(2,128)(2,1)}), bf16[64,2,3,16,128]{4,1,0,2,3:T(2,128)(2,1)S(1)}, u32[]{:S(2)}, u32[]{:S(2)}) async-start(bf16[64,2,3,16,128]{4,1,0,2,3:T(2,128)(2,1)} %copy.35), calls=%async_computation.3 | async-start | bytes 3145728 | tf_op jit(solution)/shard_map/all_to_all | solution.py:78
  237.4 1.1 copy.33
  238.5 1.3 reshape_reshape.7
  239.9 12.1 %all-to-all-done.3 = bf16[64,2,3,16,128]{4,1,0,2,3:T(2,128)(2,1)S(1)} async-done(((bf16[64,2,3,16,128]{4,1,0,2,3:T(2,128)(2,1)}), bf16[64,2,3,16,128]{4,1,0,2,3:T(2,128)(2,1)S(1)}, u32[]{:S(2)}, u32[]{:S(2)}) %all-to-all-start.3) | async-done | bytes 1572896 | tf_op jit(solution)/shard_map/all_to_all | solution.py:78
  252.0 1.1 copy.36
  253.2 12.2 %while.18 = (s32[]{:T(128)}, bf16[4,512,128]{2,1,0:T(8,128)(2,1)}, s32[4,512]{1,0:T(4,128)S(1)}, s32[64,32,1,1]{1,0,3,2:T(8,128)}, bf16[4,512,128]{2,1,0:T(8,128...) while((s32[]{:T(128)}, bf16[4,512,128]{2,1,0:T(8,128)(2,1)}, ...), condition=%wide.wide.region_4.5_spmd, body=%wide.wide.region_1.4_spmd.sunk | while | flops 545389568 | bytes 13918821 | solution.py:57
  253.2 0.9 fusion.38
  254.1 0.7 fusion.39
  254.8 1.5 fusion.40
  256.3 0.9 fusion.38
  257.2 0.7 fusion.39
  257.9 1.5 fusion.40
  259.3 0.9 fusion.38
  260.9 1.5 fusion.40
  262.4 0.9 fusion.38
  264.0 1.5 fusion.40
  265.4 23.2 %all-to-all-start.4 = ((bf16[1024,1,2,1,128]{4,2,3,1,0:T(2,128)(2,1)}), bf16[1024,1,2,1,128]{4,2,3,1,0:T(2,128)(2,1)S(1)}, u32[]{:S(2)}, u32[]{:S(2)}) async-start(bf16[1024,1,2,1,128]{4,2,3,1,0:T(2,128)(2,1)} %bitcast.82), calls=%async_computation.4 | async-start | bytes 1048576 | tf_op jit(solution)/shard_map/all_to_all | solution.py:29
  288.7 2.6 sort.35
  291.3 60.9 %all-to-all-done.4 = bf16[1024,1,2,1,128]{4,2,3,1,0:T(2,128)(2,1)S(1)} async-done(((bf16[1024,1,2,1,128]{4,2,3,1,0:T(2,128)(2,1)}), bf16[1024,1,2,1,128]{4,2,3,1,0:T(2,128)(2,1)S(1)}, u32[]{:S(2)}, u32[]{:S(2)}) %all-to-all-start.4) | async-done | bytes 524320 | tf_op jit(solution)/shard_map/all_to_all | solution.py:29
  352.5 1.7 gather_fusion.2
  (31 shorter events, 4.6 us)
Async XLA Ops:
  0.0 36.2 %copy-start = (bf16[128,3,2048]{2,0,1:T(8,128)(2,1)S(1)}, bf16[128,3,2048]{2,0,1:T(8,128)(2,1)}, u32[]{:S(2)}) copy-start(bf16[128,3,2048]{2,0,1:T(8,128)(2,1)} %param.5) | copy-start | bytes 4718596
  5.8 55.6 %all-to-all-start = ((s32[64,2,1,16]{3,1,2,0:T(2,128)}), s32[64,2,1,16]{3,1,2,0:T(2,128)S(1)}, u32[]{:S(2)}, u32[]{:S(2)}) async-start(s32[64,2,1,16]{3,1,2,0:T(2,128)} %broadcast_in_dim.31), calls=%async_computation | async-start | bytes 131072 | tf_op jit(solution)/shard_map/all_to_all | solution.py:86
  61.4 157.6 %all-to-all-start.2 = ((bf16[64,2,3,16,128]{4,3,1,2,0:T(8,128)(2,1)}), bf16[64,2,3,16,128]{4,3,1,2,0:T(8,128)(2,1)S(1)}, u32[]{:S(2)}, u32[]{:S(2)}) async-start(bf16[64,2,3,16,128]{4,3,1,2,0:T(8,128)(2,1)} %copy.34), calls=%async_computation.2 | async-start | bytes 3145728 | tf_op jit(solution)/shard_map/all_to_all | solution.py:79
  219.0 13.1 %all-to-all-start.1 = ((s32[16,1,128]{2,1,0:T(1,128)}), s32[16,1,128]{2,1,0:T(1,128)S(1)}, u32[]{:S(2)}, u32[]{:S(2)}) async-start(s32[16,1,128]{2,1,0:T(1,128)} %reshape.55), calls=%async_computation.1 | async-start | bytes 16384 | tf_op jit(solution)/shard_map/all_to_all | solution.py:85
  232.1 19.8 %all-to-all-start.3 = ((bf16[64,2,3,16,128]{4,1,0,2,3:T(2,128)(2,1)}), bf16[64,2,3,16,128]{4,1,0,2,3:T(2,128)(2,1)S(1)}, u32[]{:S(2)}, u32[]{:S(2)}) async-start(bf16[64,2,3,16,128]{4,1,0,2,3:T(2,128)(2,1)} %copy.35), calls=%async_computation.3 | async-start | bytes 3145728 | tf_op jit(solution)/shard_map/all_to_all | solution.py:78
  237.4 15.8 %copy-start.1 = (s32[64,32,1,1]{1,0,3,2:T(8,128)}, s32[64,32,1,1]{1,0,3,2:T(8,128)S(1)}, u32[]{:S(2)}) copy-start(s32[64,32,1,1]{1,0,3,2:T(8,128)S(1)} %copy.37) | copy-start | bytes 24580
  265.4 86.8 %all-to-all-start.4 = ((bf16[1024,1,2,1,128]{4,2,3,1,0:T(2,128)(2,1)}), bf16[1024,1,2,1,128]{4,2,3,1,0:T(2,128)(2,1)S(1)}, u32[]{:S(2)}, u32[]{:S(2)}) async-start(bf16[1024,1,2,1,128]{4,2,3,1,0:T(2,128)(2,1)} %bitcast.82), calls=%async_computation.4 | async-start | bytes 1048576 | tf_op jit(solution)/shard_map/all_to_all | solution.py:29
where the time goes:
time: 355 us; the launch traced here: 354 us
  waiting for transfers between devices  246 us (69%)
  starting transfers between devices  70 us (20%)
  local copies, waits for them, and re-layouts  19.6 us (6%)
  other arithmetic  9.41 us (3%)
  matrix products  9.35 us (3%)
    all_to_all x1, waiting for transfers between devices, local(): lax.all_to_all(grouped, 'bag', split_axis=0, concat_axis=0, tiled=True)  151 us
    all_to_all x1, waiting for transfers between devices, joined_exchange(): lax.all_to_all(pieces, axis, split_axis=0, concat_axis=0, tiled=True)  60.9 us
    all_to_all x1, starting transfers between devices, local(): lax.all_to_all(grouped_ids, 'bag', split_axis=0, concat_axis=0, tiled=True)  30.4 us
    all_to_all x1, starting transfers between devices, joined_exchange(): lax.all_to_all(pieces, axis, split_axis=0, concat_axis=0, tiled=True)  23.2 us
    all_to_all x1, waiting for transfers between devices, local(): lax.all_to_all(grouped_ids, 'bag', split_axis=0, concat_axis=0, tiled=True)  18.1 us
    all_to_all x1, waiting for transfers between devices, local(): lax.all_to_all(lax.all_to_all(grouped, 'bag', split_axis=0, concat_axis=0...  12.1 us
  transfers between devices with their start and end apart: 5, of which 5 were waited for; matrix products, arithmetic and copies ran while one was open for 5% of the time, Pallas kernels for 0%

commit v1 on v0

v1 whole, which is shorter than its diff:
```python
import functools
import math

import jax
import jax.numpy as jnp
from jax import lax
from jax.experimental import pallas as pl
from jax.experimental.pallas import tpu as pltpu
from jax.sharding import PartitionSpec as P

HD = 128
VIDEOS = 2
CHUNKS = 4
GROUP = 8
APART = 2.0**100
MESH = pl.DeviceIdType.MESH
F32, BF16, I32 = jnp.float32, jnp.bfloat16, jnp.int32


def reach(bag, slot, bags, way):
    chips = bags // 2
    hops = chips // 2 - lax.div(slot + 2, 4)
    side = way * (1 - 2 * lax.rem(lax.div(slot + 2, 2), 2))
    chip = lax.rem(lax.div(bag, 2) + hops * side + chips, chips)
    return chip * 2 + lax.rem(lax.rem(bag, 2) + slot + 1, 2)


def reach_rows(bag, slot, bags):
    chips = bags // 2
    hops = chips // 2 - ((slot + 2) >> 2)
    side = 1 - 2 * (((slot + 2) >> 1) & 1)
    chip = (lax.div(bag, 2) + hops * side + chips) & (chips - 1)
    return chip * 2 + ((lax.rem(bag, 2) + slot + 1) & 1)


def mat(a, b):
    return jnp.dot(a, b, preferred_element_type=F32)


def kernel(
    bags, heads, scaling,
    x_ref, ids_ref, route_ref, out_ref,
    place, place_t, mix, mix_t, picked,
    zs, zr, ys, kv, qs, qr, ka, va, qaug, oc, zos, zor, yo, home,
    bit_s, bit_r, row_s, row_r,
    zs_sem, zr_sem, zq_sem, zo_sem, xs_sem, xr_sem, xq_sem, xo_sem,
):
    bag, head = lax.axis_index("bag"), lax.axis_index("head")
    tok = x_ref.shape[1]
    last = bags - 1
    slots = bags // CHUNKS
    rows = 2 * slots
    span = 2 * GROUP
    pair = 2 * heads
    groups = slots // GROUP

    barrier = pltpu.get_barrier_semaphore()

    def greet_bag(k, carry):
        pl.semaphore_signal(
            barrier, inc=1, device_id=(reach(bag, k, bags, 1), head), device_id_type=MESH
        )
        return carry

    def greet_head(j, carry):
        pl.semaphore_signal(
            barrier, inc=1, device_id=(bag, lax.rem(head + 1 + j, heads)), device_id_type=MESH
        )
        return carry

    lax.fori_loop(0, last, greet_bag, 0)
    lax.fori_loop(0, heads - 1, greet_head, 0)

    route = route_ref[...]
    lanes = jnp.broadcast_to(route.astype(F32), (tok, tok))
    down = lax.broadcasted_iota(I32, (tok, tok), 0)
    along = lax.broadcasted_iota(I32, (tok, tok), 1)
    earlier = (lanes == lanes.T) & (down < along)
    rank = jnp.sum(jnp.where(earlier, 1.0, 0.0), axis=0, keepdims=True).astype(I32)
    hit = (reach_rows(bag, down >> 1, bags) == route) & (rank == (down & 1))
    spots = jnp.where(hit, 1.0, 0.0)
    place[...] = spots.astype(BF16)
    place_t[...] = spots.T.astype(BF16)

    side = mix.shape[0]
    mo = lax.broadcasted_iota(I32, (side, side), 0)
    mi = lax.broadcasted_iota(I32, (side, side), 1)
    h_bits = heads.bit_length() - 1

    def swapped(a):
        head_of, slot_of, pair_of = a >> 4, (a >> 1) & (GROUP - 1), a & 1
        return (slot_of << (h_bits + 1)) + head_of * 2 + pair_of

    mix[...] = jnp.where(swapped(mo) == mi, 1.0, 0.0).astype(BF16)
    mix_t[...] = jnp.where(swapped(mi) == mo, 1.0, 0.0).astype(BF16)

    slot_rows = lax.broadcasted_iota(I32, (bags, tok), 0)
    bits = (ids_ref[...] - VIDEOS * route).astype(F32)
    mine = jnp.where(reach_rows(bag, slot_rows, bags) == route, bits, 0.0)
    pick = jnp.where(rank == down, 1.0, 0.0)
    slot_bits = lax.dot_general(
        mine.astype(BF16), pick.astype(BF16), (((1,), (1,)), ((), ())), preferred_element_type=F32
    )
    bit_s[...] = slot_bits.reshape(bags, 1, tok)

    def split(i, carry):
        t = lax.rem(i + 1, 3)
        picked[...] = mat(place[...], x_ref[t]).astype(BF16)
        for g in range(bags // GROUP):
            block = jnp.concatenate(
                [picked[g * span : (g + 1) * span, h * HD : (h + 1) * HD] for h in range(heads)],
                axis=0,
            )
            spread = mat(mix_t[...], block).astype(BF16)
            zs[t, g * GROUP : (g + 1) * GROUP] = spread.reshape(GROUP, pair, HD)
        return carry

    lax.fori_loop(0, 3, split, 0)

    pl.semaphore_wait(barrier, last + heads - 1)

    def across(k, src, dst, send, recv, way):
        pltpu.make_async_remote_copy(
            src_ref=src, dst_ref=dst, send_sem=send, recv_sem=recv,
            device_id=(reach(bag, k, bags, way), head), device_id_type=MESH,
        ).start()

    def send_tensor(t, recv, lo, hi):
        def one(k, carry):
            across(k, zs.at[t, k], zr.at[t, k], zs_sem.at[t], recv, 1)
            return carry

        lax.fori_loop(lo, hi, one, 0)

    def send_bits(k, carry):
        across(k, bit_s.at[k], bit_r.at[k], zs_sem.at[3], zr_sem.at[2], 1)
        return carry

    def keep(src, dst, sem):
        pltpu.make_async_copy(src, dst, sem).start()

    def arrived(ref, sem):
        pltpu.make_async_copy(ref, ref, sem).wait()

    send_tensor(1, zr_sem.at[0], 0, last)
    keep(zs.at[1, last], zr.at[1, last], zr_sem.at[0])
    lax.fori_loop(0, last, send_bits, 0)
    keep(bit_s.at[last], bit_r.at[last], zr_sem.at[2])
    send_tensor(2, zr_sem.at[1], 0, last)
    keep(zs.at[2, last], zr.at[2, last], zr_sem.at[1])

    def send_queries(c, carry):
        send_tensor(0, zq_sem.at[c], c * slots, (c + 1) * slots - lax.div(c, CHUNKS - 1))
        return carry

    lax.fori_loop(0, CHUNKS, send_queries, 0)
    keep(zs.at[0, last], zr.at[0, last], zq_sem.at[CHUNKS - 1])

    def hand_out(src, dst, send, recv):
        def one(j, carry):
            to = lax.rem(head + 1 + j, heads)
            pltpu.make_async_remote_copy(
                src_ref=src(to), dst_ref=dst, send_sem=send, recv_sem=recv,
                device_id=(bag, to), device_id_type=MESH,
            ).start()
            return carry

        lax.fori_loop(0, heads - 1, one, 0)
        keep(src(head), dst, recv)

    def gather_kv(i):
        for g in range(bags // GROUP):
            block = zr[1 + i, g * GROUP : (g + 1) * GROUP].reshape(side, HD)
            ys[i, :, g * span : (g + 1) * span, :] = (
                mat(mix[...], block).astype(BF16).reshape(heads, span, HD)
            )
        hand_out(lambda to: ys.at[i, to], kv.at[i, head], xs_sem.at[1 + i], xr_sem.at[i])

    arrived(zr.at[1], zr_sem.at[0])
    gather_kv(0)

    arrived(bit_r, zr_sem.at[2])
    got = bit_r[...].reshape(bags, tok)
    lane = lax.broadcasted_iota(I32, (bags, tok), 1)
    spread_bits = jnp.where((lane & 1) == 0, got[:, 0:1], got[:, 1:2])
    own = lax.broadcasted_iota(I32, (bags, tok), 0) == (lane >> 1)
    row_s[...] = jnp.sum(jnp.where(own, spread_bits, 0.0), axis=0, keepdims=True)
    hand_out(lambda to: row_s, row_r.at[head], xs_sem.at[3], xr_sem.at[2])

    arrived(row_r, xr_sem.at[2])
    columns = row_r[...].reshape(heads, tok).T
    lane_row = lax.broadcasted_iota(I32, (1, HD), 1)
    first, second = lane_row == 0, lane_row == 1
    q_slope = jnp.where(first, 1.0, jnp.where(second, -1.0, 0.0))
    q_base = jnp.where(second, 1.0, 0.0)
    k_slope = q_slope * APART
    k_base = jnp.where(first, -APART, 0.0)
    for h in range(heads):
        column = columns[:, h : h + 1]
        qaug[:, h] = (column * q_slope + q_base).astype(BF16).reshape(CHUNKS, rows, HD)
        ka[h * tok : (h + 1) * tok, HD:] = (column * k_slope + k_base).astype(BF16)

    arrived(kv.at[0], xr_sem.at[0])
    ka[:, :HD] = kv[0].reshape(heads * tok, HD)

    arrived(zr.at[2], zr_sem.at[1])
    gather_kv(1)
    va[:, HD:] = jnp.broadcast_to(jnp.where(first, 1.0, 0.0), (heads * tok, HD)).astype(BF16)
    arrived(kv.at[1], xr_sem.at[1])
    va[:, :HD] = kv[1].reshape(heads * tok, HD)

    part = GROUP
    exponent = scaling * math.log2(math.e)

    def answer(c, carry):
        base = pl.multiple_of(c * slots, slots)
        arrived(zr.at[0, pl.ds(base, slots)], zq_sem.at[c])
        for j in range(groups):
            block = zr[0, pl.ds(base + j * GROUP, GROUP)].reshape(side, HD)
            qs[c, :, j * span : (j + 1) * span, :] = (
                mat(mix[...], block).astype(BF16).reshape(heads, span, HD)
            )
        hand_out(lambda to: qs.at[c, to], qr.at[c, head], xs_sem.at[0], xq_sem.at[c])
        arrived(qr.at[c], xq_sem.at[c])

        def block_of(i, inner):
            at = pl.ds(i * part, part)
            query = jnp.concatenate(
                [qr[c, at].reshape(part * rows, HD), qaug[c, at].reshape(part * rows, HD)], axis=1
            )
            scores = lax.dot_general(
                query, ka[...], (((1,), (1,)), ((), ())), preferred_element_type=F32
            )
            row_max = jnp.max(scores, axis=1, keepdims=True)
            probs = jnp.exp2((scores - row_max) * exponent).astype(BF16)
            mixed = mat(probs, va[...])
            result = (mixed[:, :HD] / mixed[:, HD : HD + 1]).astype(BF16)
            oc[at] = result.reshape(part, rows, HD)
            return inner

        lax.fori_loop(0, heads // part, block_of, 0)
        for j in range(groups):
            block = oc[:, j * span : (j + 1) * span, :].reshape(side, HD)
            zos[pl.ds(base + j * GROUP, GROUP)] = (
                mat(mix_t[...], block).astype(BF16).reshape(GROUP, pair, HD)
            )

        def give_back(k, inner):
            across(k, zos.at[k], zor.at[k], zs_sem.at[4], zo_sem.at[c], -1)
            return inner

        lax.fori_loop(c * slots, (c + 1) * slots - lax.div(c, CHUNKS - 1), give_back, 0)
        return carry

    lax.fori_loop(0, CHUNKS, answer, 0)
    keep(zos.at[last], zor.at[last], zo_sem.at[CHUNKS - 1])

    def collect(c, carry):
        base = pl.multiple_of(c * slots, slots)
        arrived(zor.at[pl.ds(base, slots)], zo_sem.at[c])
        for j in range(groups):
            block = zor[pl.ds(base + j * GROUP, GROUP)].reshape(side, HD)
            yo[c, :, j * span : (j + 1) * span, :] = (
                mat(mix[...], block).astype(BF16).reshape(heads, span, HD)
            )
        hand_out(
            lambda to: yo.at[c, to],
            home.at[c, :, pl.ds(pl.multiple_of(head * HD, HD), HD)],
            xs_sem.at[4],
            xo_sem.at[c],
        )
        return carry

    lax.fori_loop(0, CHUNKS, collect, 0)

    def landed(c, carry):
        arrived(home.at[c], xo_sem.at[c])
        return carry

    lax.fori_loop(0, CHUNKS, landed, 0)
    out_ref[...] = mat(place_t[...], home[...].reshape(tok, heads * HD)).astype(BF16)

    for t in range(3):
        arrived(zs.at[t, pl.ds(0, last)], zs_sem.at[t])
    arrived(bit_s.at[pl.ds(0, last)], zs_sem.at[3])
    arrived(zos.at[pl.ds(0, last)], zs_sem.at[4])
    arrived(qs.at[:, pl.ds(0, heads - 1)], xs_sem.at[0])
    for i in range(2):
        arrived(ys.at[i, pl.ds(0, heads - 1)], xs_sem.at[1 + i])
    arrived(row_r.at[pl.ds(0, heads - 1)], xs_sem.at[3])
    arrived(yo.at[:, pl.ds(0, heads - 1)], xs_sem.at[4])


def local(bags, heads, projected, video_ids, bag_route):
    tok, _, feat = projected.shape
    slots = bags // CHUNKS
    rows = 2 * slots
    bag_rows = heads * tok
    side = GROUP * 2 * heads
    vm, dma = pltpu.VMEM, pltpu.SemaphoreType.DMA
    return pl.pallas_call(
        functools.partial(kernel, bags, heads, 1.0 / math.sqrt(HD)),
        out_shape=jax.ShapeDtypeStruct((tok, feat), BF16),
        in_specs=[pl.BlockSpec(memory_space=pltpu.VMEM)] * 3,
        out_specs=pl.BlockSpec(memory_space=pltpu.VMEM),
        scratch_shapes=[
            vm((tok, tok), BF16),
            vm((tok, tok), BF16),
            vm((side, side), BF16),
            vm((side, side), BF16),
            vm((tok, feat), BF16),
            vm((3, bags, 2 * heads, HD), BF16),
            vm((3, bags, 2 * heads, HD), BF16),
            vm((2, heads, tok, HD), BF16),
            vm((2, heads, tok, HD), BF16),
            vm((CHUNKS, heads, rows, HD), BF16),
            vm((CHUNKS, heads, rows, HD), BF16),
            vm((bag_rows, 2 * HD), BF16),
            vm((bag_rows, 2 * HD), BF16),
            vm((CHUNKS, heads, rows, HD), BF16),
            vm((heads, rows, HD), BF16),
            vm((bags, 2 * heads, HD), BF16),
            vm((bags, 2 * heads, HD), BF16),
            vm((CHUNKS, heads, rows, HD), BF16),
            vm((CHUNKS, rows, feat), BF16),
            vm((bags, 1, tok), F32),
            vm((bags, 1, tok), F32),
            vm((1, tok), F32),
            vm((heads, 1, tok), F32),
            dma((5,)),
            dma((3,)),
            dma((CHUNKS,)),
            dma((CHUNKS,)),
            dma((5,)),
            dma((3,)),
            dma((CHUNKS,)),
            dma((CHUNKS,)),
        ],
        compiler_params=pltpu.CompilerParams(
            collective_id=0, has_side_effects=True, vmem_limit_bytes=48 << 20
        ),
        name="routed_attention",
    )(jnp.transpose(projected, (1, 0, 2)), video_ids.reshape(1, tok), bag_route.reshape(1, tok))


def solution(mesh):
    placed = (P(("bag", "head"), None, None), P(("bag", "head")), P(("bag", "head")))
    return jax.shard_map(
        functools.partial(local, mesh.shape["bag"], mesh.shape["head"]),
        mesh=mesh,
        in_specs=placed,
        out_specs=P(("bag", "head"), None),
        check_vma=False,
    )
```

time: 355 us -> 225 us (0.63)
  waiting for transfers between devices: 246 us -> 0 us
  Pallas kernels: 0 us -> 222 us
  starting transfers between devices: 70 us -> 0 us
  local copies, waits for them, and re-layouts: 19.6 us -> 3.51 us
  other arithmetic: 9.41 us -> 0 us
  matrix products: 9.35 us -> 0 us
    all_to_all x5 -> x0, waiting for transfers between devices: 246 us -> none  [the longest x1 151 us: local(): lax.all_to_all(grouped, 'bag', split_axis=0, concat_axis=0, tiled=True)]
    pallas_call x0 -> x1, Pallas kernels: none -> 222 us  [local(): pl.pallas_call(functools.partial(kernel, bags, heads, 1.0 / math.sqrt(HD)...]
    all_to_all x5 -> x0, starting transfers between devices: 70 us -> none  [the longest x1 30.4 us: local(): lax.all_to_all(grouped_ids, 'bag', split_axis=0, concat_axis=0, tiled=True)]
    dot_general x8 -> x0, matrix products: 9.35 us -> none  [the longest x4 5.81 us: one_block(): jnp.dot(weights.astype(jnp.bfloat16), value_rows, preferred_element_type=...]
    gather x3 -> x0, local copies, waits for them, and re-layouts: 8.51 us -> none  [the longest x1 5.2 us: local(): projected[ordering].reshape(bag_count, per_bag, 3, head_count, head_width)]
    sort x2 -> x0, other arithmetic: 5.92 us -> none  [the longest x1 3.3 us: local(): ordering = jnp.argsort(bag_route, stable=True)]
    all_to_all x7 -> x0, local copies, waits for them, and re-layouts: 5.73 us -> none  [the longest x1 2.86 us: local(): lax.all_to_all(grouped, 'bag', split_axis=0, concat_axis=0, tiled=True)]
  transfers between devices with their start and end apart: 5 -> 0, of which waited for: 5 -> 0; matrix products, arithmetic and copies ran while one was open for 5% -> 0% of each run, Pallas kernels for 0% -> 0%
where the time goes in v1:
time: 225 us
  Pallas kernels  222 us (99%)
  local copies, waits for them, and re-layouts  3.51 us (2%)
    pallas_call x1, Pallas kernels, local(): pl.pallas_call(functools.partial(kernel, bags, heads, 1.0 / math.sqrt(HD)...  222 us

profile of v1, /device:TPU:1, one launch (start us, length us, event | category | flops | bytes accessed | tf_op | source)
XLA Modules:
  0.0 225.0 jit_solution(1938447069770137217)
XLA Ops:
  0.0 0.0 copy-start
  0.0 1.4 copy-done
  1.4 0.0 copy-start.1
  1.4 0.7 copy-done.1
  2.1 0.0 copy-start.2
  2.1 0.7 copy-done.2
  2.7 221.5 %routed_attention.1 = bf16[128,2048]{1,0:T(8,128)(2,1)S(1)} custom-call(bf16[3,128,2048]{2,1,0:T(8,128)(2,1)S(1)} %bitcast.3, s32[1,128]{1,0:T(1,128)S(1)} %bitcast.4, s32[1,128]{1,0:T(1,128)S(1)} %bitcast.5), custom_call_target="tpu_custom_call" | custom-call | tf_op jit(solution)/shard_map/routed_attention/pallas_call | solution.py:301
  224.2 0.8 copy.5
Async XLA Ops:
  0.0 1.4 copy-start
  1.4 0.7 copy-start.1
  2.1 0.7 copy-start.2

commit v2 on v1

--- a/solution.py
+++ b/solution.py
@@ -39,11 +39,12 @@
 
 def kernel(
     bags, heads, scaling,
-    x_ref, ids_ref, route_ref, out_ref,
+    x_hbm, ids_hbm, route_hbm, out_ref,
+    x_ref, ids_ref, route_ref,
     place, place_t, mix, mix_t, picked,
-    zs, zr, ys, kv, qs, qr, ka, va, qaug, oc, zos, zor, yo, home,
-    bit_s, bit_r, row_s, row_r,
-    zs_sem, zr_sem, zq_sem, zo_sem, xs_sem, xr_sem, xq_sem, xo_sem,
+    zs, zr, ys, kv, qs, qr, ka, va, qaug, oc, oc_in, zos, zor, home,
+    row_s, row_r, bit_s, bit_r, all_bits,
+    zs_sem, zr_sem, zq_sem, zo_sem, xs_sem, xr_sem, xq_sem, xo_sem, in_sem, wave,
 ):
     bag, head = lax.axis_index("bag"), lax.axis_index("head")
     tok = x_ref.shape[1]
@@ -54,22 +55,30 @@
     pair = 2 * heads
     groups = slots // GROUP
 
+    chips = bags // 2
+    chip, core = lax.div(bag, 2), lax.rem(bag, 2)
+    above, below = lax.rem(chip + 1, chips) * 2, lax.rem(chip + chips - 1, chips) * 2
+
     barrier = pltpu.get_barrier_semaphore()
 
-    def greet_bag(k, carry):
-        pl.semaphore_signal(
-            barrier, inc=1, device_id=(reach(bag, k, bags, 1), head), device_id_type=MESH
-        )
-        return carry
-
-    def greet_head(j, carry):
-        pl.semaphore_signal(
-            barrier, inc=1, device_id=(bag, lax.rem(head + 1 + j, heads)), device_id_type=MESH
-        )
-        return carry
-
-    lax.fori_loop(0, last, greet_bag, 0)
-    lax.fori_loop(0, heads - 1, greet_head, 0)
+    def greet(to_bag, to_head):
+        pl.semaphore_signal(barrier, inc=1, device_id=(to_bag, to_head), device_id_type=MESH)
+
+    for near in (above, below):
+        greet(near, head)
+        greet(near + 1, head)
+    greet(chip * 2 + 1 - core, head)
+    for j in range(1, heads):
+        greet(bag, lax.rem(head + j, heads))
+
+    loads = [
+        pltpu.make_async_copy(route_hbm, route_ref, in_sem.at[3]),
+        pltpu.make_async_copy(ids_hbm, ids_ref, in_sem.at[4]),
+    ] + [pltpu.make_async_copy(x_hbm.at[t], x_ref.at[t], in_sem.at[t]) for t in (1, 2, 0)]
+    for load in loads:
+        load.start()
+    loads[0].wait()
+    loads[1].wait()
 
     route = route_ref[...]
     lanes = jnp.broadcast_to(route.astype(F32), (tok, tok))
@@ -94,30 +103,27 @@
     mix[...] = jnp.where(swapped(mo) == mi, 1.0, 0.0).astype(BF16)
     mix_t[...] = jnp.where(swapped(mi) == mo, 1.0, 0.0).astype(BF16)
 
-    slot_rows = lax.broadcasted_iota(I32, (bags, tok), 0)
     bits = (ids_ref[...] - VIDEOS * route).astype(F32)
-    mine = jnp.where(reach_rows(bag, slot_rows, bags) == route, bits, 0.0)
-    pick = jnp.where(rank == down, 1.0, 0.0)
-    slot_bits = lax.dot_general(
-        mine.astype(BF16), pick.astype(BF16), (((1,), (1,)), ((), ())), preferred_element_type=F32
-    )
-    bit_s[...] = slot_bits.reshape(bags, 1, tok)
-
-    def split(i, carry):
-        t = lax.rem(i + 1, 3)
+    row_s[...] = mat(jnp.broadcast_to(bits, (8, tok)).astype(BF16), place_t[...])[0:1]
+
+    def split(t):
+        pltpu.make_async_copy(x_hbm.at[t], x_ref.at[t], in_sem.at[t]).wait()
         picked[...] = mat(place[...], x_ref[t]).astype(BF16)
-        for g in range(bags // GROUP):
+
+        def spread(g, carry):
+            lines = pl.ds(pl.multiple_of(g * span, span), span)
             block = jnp.concatenate(
-                [picked[g * span : (g + 1) * span, h * HD : (h + 1) * HD] for h in range(heads)],
-                axis=0,
-            )
-            spread = mat(mix_t[...], block).astype(BF16)
-            zs[t, g * GROUP : (g + 1) * GROUP] = spread.reshape(GROUP, pair, HD)
-        return carry
-
-    lax.fori_loop(0, 3, split, 0)
-
-    pl.semaphore_wait(barrier, last + heads - 1)
+                [picked[lines, h * HD : (h + 1) * HD] for h in range(heads)], axis=0
+            )
+            zs[t, pl.ds(g * GROUP, GROUP)] = (
+                mat(mix_t[...], block).astype(BF16).reshape(GROUP, pair, HD)
+            )
+            return carry
+
+        lax.fori_loop(0, bags // GROUP, spread, 0, unroll=4)
+
+    split(1)
+    pl.semaphore_wait(barrier, 5 + heads - 1)
 
     def across(k, src, dst, send, recv, way):
         pltpu.make_async_remote_copy(
@@ -132,29 +138,11 @@
 
         lax.fori_loop(lo, hi, one, 0)
 
-    def send_bits(k, carry):
-        across(k, bit_s.at[k], bit_r.at[k], zs_sem.at[3], zr_sem.at[2], 1)
-        return carry
-
     def keep(src, dst, sem):
         pltpu.make_async_copy(src, dst, sem).start()
 
     def arrived(ref, sem):
         pltpu.make_async_copy(ref, ref, sem).wait()
-
-    send_tensor(1, zr_sem.at[0], 0, last)
-    keep(zs.at[1, last], zr.at[1, last], zr_sem.at[0])
-    lax.fori_loop(0, last, send_bits, 0)
-    keep(bit_s.at[last], bit_r.at[last], zr_sem.at[2])
-    send_tensor(2, zr_sem.at[1], 0, last)
-    keep(zs.at[2, last], zr.at[2, last], zr_sem.at[1])
-
-    def send_queries(c, carry):
-        send_tensor(0, zq_sem.at[c], c * slots, (c + 1) * slots - lax.div(c, CHUNKS - 1))
-        return carry
-
-    lax.fori_loop(0, CHUNKS, send_queries, 0)
-    keep(zs.at[0, last], zr.at[0, last], zq_sem.at[CHUNKS - 1])
 
     def hand_out(src, dst, send, recv):
         def one(j, carry):
@@ -168,6 +156,74 @@
         lax.fori_loop(0, heads - 1, one, 0)
         keep(src(head), dst, recv)
 
+    hand_out(lambda to: row_s, row_r.at[head], xs_sem.at[3], xr_sem.at[2])
+
+    send_tensor(1, zr_sem.at[0], last - 1, last)
+
+    def widen(stage, carry):
+        first_slot = 4 * (chips // 2 - stage) - 2
+        for i in range(4):
+            k = first_slot + i
+            across(k, zs.at[1, k], zr.at[1, k], zs_sem.at[1], zr_sem.at[0], 1)
+        for i, near in enumerate((below, above)):
+            pl.semaphore_signal(
+                wave.at[i], inc=1, device_id=(near + core, head), device_id_type=MESH
+            )
+        pl.semaphore_wait(wave.at[0], 1)
+        pl.semaphore_wait(wave.at[1], 1)
+        return carry
+
+    lax.fori_loop(1, chips // 2, widen, 0)
+    send_tensor(1, zr_sem.at[0], 0, 2)
+    keep(zs.at[1, last], zr.at[1, last], zr_sem.at[0])
+
+    share = bags // heads
+    arrived(row_r, xr_sem.at[2])
+    rows_in = row_r[...].reshape(heads, tok)
+    odd = lax.broadcasted_iota(I32, (heads, tok), 1) & 1
+    stacked = jnp.concatenate(
+        [
+            jnp.where(odd == 0, rows_in, 0.0),
+            jnp.where(odd == 1, rows_in, 0.0),
+            jnp.zeros((tok - 2 * heads, tok), F32),
+        ],
+        axis=0,
+    )
+    slot_at = lax.broadcasted_iota(I32, (bags, tok), 0)
+    lane_at = lax.broadcasted_iota(I32, (bags, tok), 1)
+    fold = jnp.where(slot_at == (lane_at >> 1), 1.0, 0.0)
+    slot_bits = lax.dot_general(
+        fold.astype(BF16), stacked.astype(BF16), (((1,), (1,)), ((), ())), preferred_element_type=F32
+    )
+    bit_s[...] = slot_bits.reshape(bags, 1, tok)
+
+    def send_bits(j, carry):
+        k = head + heads * j
+        across(k, bit_s.at[k], bit_r.at[j], zs_sem.at[3], zr_sem.at[2], 1)
+        return carry
+
+    lax.fori_loop(0, share - 1, send_bits, 0)
+
+    @pl.when(head < heads - 1)
+    def _():
+        send_bits(share - 1, 0)
+
+    @pl.when(head == heads - 1)
+    def _():
+        keep(bit_s.at[last], bit_r.at[share - 1], zr_sem.at[2])
+
+    split(2)
+    send_tensor(2, zr_sem.at[1], 0, last)
+    keep(zs.at[2, last], zr.at[2, last], zr_sem.at[1])
+    split(0)
+
+    def send_queries(c, carry):
+        send_tensor(0, zq_sem.at[c], c * slots, (c + 1) * slots - lax.div(c, CHUNKS - 1))
+        return carry
+
+    lax.fori_loop(0, CHUNKS, send_queries, 0)
+    keep(zs.at[0, last], zr.at[0, last], zq_sem.at[CHUNKS - 1])
+
     def gather_kv(i):
         for g in range(bags // GROUP):
             block = zr[1 + i, g * GROUP : (g + 1) * GROUP].reshape(side, HD)
@@ -180,15 +236,20 @@
     gather_kv(0)
 
     arrived(bit_r, zr_sem.at[2])
-    got = bit_r[...].reshape(bags, tok)
-    lane = lax.broadcasted_iota(I32, (bags, tok), 1)
-    spread_bits = jnp.where((lane & 1) == 0, got[:, 0:1], got[:, 1:2])
-    own = lax.broadcasted_iota(I32, (bags, tok), 0) == (lane >> 1)
-    row_s[...] = jnp.sum(jnp.where(own, spread_bits, 0.0), axis=0, keepdims=True)
-    hand_out(lambda to: row_s, row_r.at[head], xs_sem.at[3], xr_sem.at[2])
-
-    arrived(row_r, xr_sem.at[2])
-    columns = row_r[...].reshape(heads, tok).T
+    hand_out(
+        lambda to: bit_r, all_bits.at[pl.ds(head * share, share)], xs_sem.at[5], xr_sem.at[3]
+    )
+    arrived(all_bits, xr_sem.at[3])
+    row_at = lax.broadcasted_iota(I32, (tok, bags), 0)
+    from_at = lax.broadcasted_iota(I32, (tok, bags), 1)
+    s_bits = share.bit_length() - 1
+    named = (from_at >> s_bits) + heads * (from_at & (share - 1))
+    wide = mat(
+        jnp.where(named == (row_at >> 1), 1.0, 0.0).astype(BF16),
+        all_bits[...].reshape(bags, tok).astype(BF16),
+    )
+    even = (lax.broadcasted_iota(I32, (tok, heads), 0) & 1) == 0
+    columns = jnp.where(even, wide[:, :heads], wide[:, heads : 2 * heads])
     lane_row = lax.broadcasted_iota(I32, (1, HD), 1)
     first, second = lane_row == 0, lane_row == 1
     q_slope = jnp.where(first, 1.0, jnp.where(second, -1.0, 0.0))
@@ -235,12 +296,14 @@
             probs = jnp.exp2((scores - row_max) * exponent).astype(BF16)
             mixed = mat(probs, va[...])
             result = (mixed[:, :HD] / mixed[:, HD : HD + 1]).astype(BF16)
-            oc[at] = result.reshape(part, rows, HD)
+            oc[c, at] = result.reshape(part, rows, HD)
             return inner
 
         lax.fori_loop(0, heads // part, block_of, 0)
+        hand_out(lambda to: oc.at[c, to], oc_in.at[c, head], xs_sem.at[4], xo_sem.at[c])
+        arrived(oc_in.at[c], xo_sem.at[c])
         for j in range(groups):
-            block = oc[:, j * span : (j + 1) * span, :].reshape(side, HD)
+            block = oc_in[c, :, j * span : (j + 1) * span, :].reshape(side, HD)
             zos[pl.ds(base + j * GROUP, GROUP)] = (
                 mat(mix_t[...], block).astype(BF16).reshape(GROUP, pair, HD)
             )
@@ -260,35 +323,31 @@
         arrived(zor.at[pl.ds(base, slots)], zo_sem.at[c])
         for j in range(groups):
             block = zor[pl.ds(base + j * GROUP, GROUP)].reshape(side, HD)
-            yo[c, :, j * span : (j + 1) * span, :] = (
-                mat(mix[...], block).astype(BF16).reshape(heads, span, HD)
-            )
-        hand_out(
-            lambda to: yo.at[c, to],
-            home.at[c, :, pl.ds(pl.multiple_of(head * HD, HD), HD)],
-            xs_sem.at[4],
-            xo_sem.at[c],
-        )
+            sorted_rows = mat(mix[...], block).astype(BF16)
+            for h in range(heads):
+                home[c, j * span : (j + 1) * span, h * HD : (h + 1) * HD] = sorted_rows[
+                    h * span : (h + 1) * span
+                ]
         return carry
 
     lax.fori_loop(0, CHUNKS, collect, 0)
-
-    def landed(c, carry):
-        arrived(home.at[c], xo_sem.at[c])
-        return carry
-
-    lax.fori_loop(0, CHUNKS, landed, 0)
     out_ref[...] = mat(place_t[...], home[...].reshape(tok, heads * HD)).astype(BF16)
 
     for t in range(3):
         arrived(zs.at[t, pl.ds(0, last)], zs_sem.at[t])
-    arrived(bit_s.at[pl.ds(0, last)], zs_sem.at[3])
+    arrived(bit_s.at[pl.ds(0, share - 1)], zs_sem.at[3])
+
+    @pl.when(head < heads - 1)
+    def _():
+        arrived(bit_s.at[last], zs_sem.at[3])
+
     arrived(zos.at[pl.ds(0, last)], zs_sem.at[4])
     arrived(qs.at[:, pl.ds(0, heads - 1)], xs_sem.at[0])
     for i in range(2):
         arrived(ys.at[i, pl.ds(0, heads - 1)], xs_sem.at[1 + i])
     arrived(row_r.at[pl.ds(0, heads - 1)], xs_sem.at[3])
-    arrived(yo.at[:, pl.ds(0, heads - 1)], xs_sem.at[4])
+    arrived(all_bits.at[pl.ds(0, bags - share)], xs_sem.at[5])
+    arrived(oc.at[:, pl.ds(0, heads - 1)], xs_sem.at[4])
 
 
 def local(bags, heads, projected, video_ids, bag_route):
@@ -301,9 +360,12 @@
     return pl.pallas_call(
         functools.partial(kernel, bags, heads, 1.0 / math.sqrt(HD)),
         out_shape=jax.ShapeDtypeStruct((tok, feat), BF16),
-        in_specs=[pl.BlockSpec(memory_space=pltpu.VMEM)] * 3,
+        in_specs=[pl.BlockSpec(memory_space=pltpu.HBM)] * 3,
         out_specs=pl.BlockSpec(memory_space=pltpu.VMEM),
         scratch_shapes=[
+            vm((3, tok, feat), BF16),
+            vm((1, tok), I32),
+            vm((1, tok), I32),
             vm((tok, tok), BF16),
             vm((tok, tok), BF16),
             vm((side, side), BF16),
@@ -318,27 +380,28 @@
             vm((bag_rows, 2 * HD), BF16),
             vm((bag_rows, 2 * HD), BF16),
             vm((CHUNKS, heads, rows, HD), BF16),
-            vm((heads, rows, HD), BF16),
+            vm((CHUNKS, heads, rows, HD), BF16),
+            vm((CHUNKS, heads, rows, HD), BF16),
             vm((bags, 2 * heads, HD), BF16),
             vm((bags, 2 * heads, HD), BF16),
-            vm((CHUNKS, heads, rows, HD), BF16),
             vm((CHUNKS, rows, feat), BF16),
-            vm((bags, 1, tok), F32),
-            vm((bags, 1, tok), F32),
             vm((1, tok), F32),
             vm((heads, 1, tok), F32),
+            vm((bags, 1, tok), F32),
+            vm((bags // heads, 1, tok), F32),
+            vm((bags, 1, tok), F32),
             dma((5,)),
             dma((3,)),
             dma((CHUNKS,)),
             dma((CHUNKS,)),
-            dma((5,)),
-            dma((3,)),
+            dma((6,)),
+            dma((4,)),
             dma((CHUNKS,)),
             dma((CHUNKS,)),
+            dma((5,)),
+            pltpu.SemaphoreType.REGULAR((2,)),
         ],
-        compiler_params=pltpu.CompilerParams(
-            collective_id=0, has_side_effects=True, vmem_limit_bytes=48 << 20
-        ),
+        compiler_params=pltpu.CompilerParams(collective_id=0, has_side_effects=True),
         name="routed_attention",
     )(jnp.transpose(projected, (1, 0, 2)), video_ids.reshape(1, tok), bag_route.reshape(1, tok))
 

time: 225 us -> 215 us (0.956)
  Pallas kernels: 222 us -> 213 us
    pallas_call x1, Pallas kernels: 222 us -> 213 us  [local(): pl.pallas_call(functools.partial(kernel, bags, heads, 1.0 / math.sqrt(HD)...]
where the time goes in v2:
time: 215 us
  Pallas kernels  213 us (99%)
    pallas_call x1, Pallas kernels, local(): pl.pallas_call(functools.partial(kernel, bags, heads, 1.0 / math.sqrt(HD)...  213 us

profile of v2, /device:TPU:1, one launch (start us, length us, event | category | flops | bytes accessed | tf_op | source)
XLA Modules:
  0.0 215.1 jit_solution(7922298842730103887)
XLA Ops:
  0.0 213.2 %routed_attention.1 = bf16[128,2048]{1,0:T(8,128)(2,1)} custom-call(bf16[3,128,2048]{2,1,0:T(8,128)(2,1)} %bitcast.3, s32[1,128]{1,0:T(1,128)} %bitcast.4, s32[1,128]{1,0:T(1,128)} %bitcast.5), custom_call_target="tpu_custom_call" | custom-call | tf_op jit(solution)/shard_map/routed_attention/pallas_call | solution.py:360
  213.2 1.9 copy.5

commit v3 on v2

--- a/solution.py
+++ b/solution.py
@@ -39,10 +39,10 @@
 
 def kernel(
     bags, heads, scaling,
-    x_hbm, ids_hbm, route_hbm, out_ref,
+    x_hbm, ids_hbm, route_hbm, home, place_out,
     x_ref, ids_ref, route_ref,
     place, place_t, mix, mix_t, picked,
-    zs, zr, ys, kv, qs, qr, ka, va, qaug, oc, oc_in, zos, zor, home,
+    zs, zr, ys, kv, qs, qr, ka, va, qaug, oc, oc_in, zos, zor,
     row_s, row_r, bit_s, bit_r, all_bits,
     zs_sem, zr_sem, zq_sem, zo_sem, xs_sem, xr_sem, xq_sem, xo_sem, in_sem, wave,
 ):
@@ -90,6 +90,7 @@
     spots = jnp.where(hit, 1.0, 0.0)
     place[...] = spots.astype(BF16)
     place_t[...] = spots.T.astype(BF16)
+    place_out[...] = place_t[...]
 
     side = mix.shape[0]
     mo = lax.broadcasted_iota(I32, (side, side), 0)
@@ -273,7 +274,7 @@
     part = GROUP
     exponent = scaling * math.log2(math.e)
 
-    def answer(c, carry):
+    def take(c):
         base = pl.multiple_of(c * slots, slots)
         arrived(zr.at[0, pl.ds(base, slots)], zq_sem.at[c])
         for j in range(groups):
@@ -282,6 +283,11 @@
                 mat(mix[...], block).astype(BF16).reshape(heads, span, HD)
             )
         hand_out(lambda to: qs.at[c, to], qr.at[c, head], xs_sem.at[0], xq_sem.at[c])
+
+    take(0)
+
+    def answer(c, carry):
+        base = pl.multiple_of(c * slots, slots)
         arrived(qr.at[c], xq_sem.at[c])
 
         def block_of(i, inner):
@@ -301,6 +307,11 @@
 
         lax.fori_loop(0, heads // part, block_of, 0)
         hand_out(lambda to: oc.at[c, to], oc_in.at[c, head], xs_sem.at[4], xo_sem.at[c])
+
+        @pl.when(c < CHUNKS - 1)
+        def _():
+            take(c + 1)
+
         arrived(oc_in.at[c], xo_sem.at[c])
         for j in range(groups):
             block = oc_in[c, :, j * span : (j + 1) * span, :].reshape(side, HD)
@@ -331,7 +342,6 @@
         return carry
 
     lax.fori_loop(0, CHUNKS, collect, 0)
-    out_ref[...] = mat(place_t[...], home[...].reshape(tok, heads * HD)).astype(BF16)
 
     for t in range(3):
         arrived(zs.at[t, pl.ds(0, last)], zs_sem.at[t])
@@ -357,11 +367,14 @@
     bag_rows = heads * tok
     side = GROUP * 2 * heads
     vm, dma = pltpu.VMEM, pltpu.SemaphoreType.DMA
-    return pl.pallas_call(
+    rested, order = pl.pallas_call(
         functools.partial(kernel, bags, heads, 1.0 / math.sqrt(HD)),
-        out_shape=jax.ShapeDtypeStruct((tok, feat), BF16),
+        out_shape=(
+            jax.ShapeDtypeStruct((CHUNKS, rows, feat), BF16),
+            jax.ShapeDtypeStruct((tok, tok), BF16),
+        ),
         in_specs=[pl.BlockSpec(memory_space=pltpu.HBM)] * 3,
-        out_specs=pl.BlockSpec(memory_space=pltpu.VMEM),
+        out_specs=[pl.BlockSpec(memory_space=pltpu.VMEM)] * 2,
         scratch_shapes=[
             vm((3, tok, feat), BF16),
             vm((1, tok), I32),
@@ -384,7 +397,6 @@
             vm((CHUNKS, heads, rows, HD), BF16),
             vm((bags, 2 * heads, HD), BF16),
             vm((bags, 2 * heads, HD), BF16),
-            vm((CHUNKS, rows, feat), BF16),
             vm((1, tok), F32),
             vm((heads, 1, tok), F32),
             vm((bags, 1, tok), F32),
@@ -404,6 +416,7 @@
         compiler_params=pltpu.CompilerParams(collective_id=0, has_side_effects=True),
         name="routed_attention",
     )(jnp.transpose(projected, (1, 0, 2)), video_ids.reshape(1, tok), bag_route.reshape(1, tok))
+    return mat(order, rested.reshape(tok, feat)).astype(BF16)
 
 
 def solution(mesh):

time: 215 us -> 213 us (level)
  no operation moved by 1% of the time
where the time goes in v3:
time: 213 us
  Pallas kernels  211 us (99%)
  matrix products  2.14 us (1%)
    pallas_call x1, Pallas kernels, local(): pl.pallas_call(functools.partial(kernel, bags, heads, 1.0 / math.sqrt(HD)...  211 us

profile of v3, /device:TPU:1, one launch (start us, length us, event | category | flops | bytes accessed | tf_op | source)
XLA Modules:
  0.0 213.2 jit_solution(12790047853610780457)
XLA Ops:
  0.0 211.1 %routed_attention.1 = (bf16[4,32,2048]{2,1,0:T(8,128)(2,1)}, bf16[128,128]{1,0:T(8,128)(2,1)}) custom-call(bf16[3,128,2048]{2,1,0:T(8,128)(2,1)} %bitcast.6, s32[1,128]{1,0:T(1,128)} %bitcast.8, s32[1,128]{1,0:T(1,128)} %bitcast.9), custom_call_target="tpu_custom_call" | custom-call | tf_op jit(solution)/shard_map/routed_attention/pallas_call | solution.py:370
  211.1 2.1 %convolution_convert_fusion = bf16[128,2048]{1,0:T(8,128)(2,1)} fusion(bf16[128,128]{1,0:T(8,128)(2,1)} %get-tuple-element.7, bf16[128,2048]{1,0:T(8,128)(2,1)} %bitcast.7), kind=kOutput, calls=%fused_computation | convolution fusion | flops 67371008 | bytes 1081344 | tf_op jit(solution)/shard_map/dot_general | solution.py:37
